TPU v7x, 128 devices: a whole 4x4x4 slice. The times are simulated.
128 devices in a mesh: ctx: 32 (over z_lo, y, x), dp: 4 (over z_hi, core).
Axes of the slice: x: 4, y: 4, z: 4 (z_hi: 2, z_lo: 2; z = z_hi * 2 + z_lo), core: 2. Of those that a mesh axis runs over, the one named last changes fastest.
Arguments:
- tokens: bfloat16 [4, 12288, 4096], P('dp', 'ctx'), may hold values from -6 to 6
- key_input: bfloat16 [4, 12288, 2048], P('dp', 'ctx'), may hold values from -6 to 6
- values: bfloat16 [4, 12288, 2048], P('dp', 'ctx'), may hold values from -6 to 6
- q_weight: bfloat16 [4096, 2048], P(('ctx', 'dp')), may hold values from -0.09375 to 0.09375
- q_spikes: int32 [4, 12288, 2048], P('dp', 'ctx'), may hold values 0 or 1
- k_spikes: int32 [4, 12288, 2048], P('dp', 'ctx'), may hold values 0 or 1
- cotangent: bfloat16 [4, 12288, 2048], P('dp', 'ctx'), may hold values from -6 to 6
Outputs:
- attended: bfloat16 [4, 12288, 2048], P('dp', 'ctx')
- grad_tokens: bfloat16 [4, 12288, 4096], P('dp', 'ctx')
- grad_keys: bfloat16 [4, 12288, 2048], P('dp', 'ctx')
- grad_values: bfloat16 [4, 12288, 2048], P('dp', 'ctx')
All inputs are finite; a program needn't handle non-finite values. No bound on the sum of `q_spikes` or of `k_spikes` on one device may be relied on, other than what follows from the above.
Results may differ from a plain program's by a relative error of at most 0.005.
Values may be sent and summed in bfloat16 or wider, within the bound.
A program may use at most 256 MiB of HBM per device.

v0:
```python
import math
import jax
import jax.numpy as jnp
from jax import lax
from jax.sharding import PartitionSpec as P

HEADS = 16
HEAD = 128
exact_mode = lax.Precision.HIGHEST


def entering(part, axis, combine, identity, reverse):
    count = lax.axis_size(axis)
    place = lax.axis_index(axis)
    ahead = count - 1 - place if reverse else place
    gathered = lax.all_gather(part, axis)
    state = jnp.zeros_like(part) + jnp.asarray(identity, part.dtype)

    def one(lap, state):
        source = count - 1 - lap if reverse else lap
        return combine(state, lax.dynamic_index_in_dim(gathered, source, 0, False))

    return lax.fori_loop(0, ahead, one, state)


def add_states(first_part, second_part):
    return first_part + second_part


def per_device(tokens, key_input, values, q_weight, q_spikes, k_spikes, cotangent):
    batches, length, model_width = tokens.shape
    head_total = q_weight.shape[1]
    sequence = length * lax.axis_size("ctx")
    factor = 3.0 / math.sqrt(HEAD * sequence)
    token_rows = tokens.reshape(batches * length, model_width)
    projected = jnp.dot(
        token_rows,
        lax.all_gather(q_weight, ("ctx", "dp"), axis=0, tiled=True),
        preferred_element_type=jnp.float32,
    )
    queries = (
        projected.reshape(batches, length, head_total) * q_spikes.astype(jnp.float32)
    ).astype(jnp.bfloat16)
    spiked_keys = key_input * k_spikes.astype(jnp.bfloat16)

    def by_heads(array):
        return array.reshape(batches, length, HEADS, HEAD)

    query_wide = by_heads(queries)
    key_wide = by_heads(spiked_keys)
    value_wide = by_heads(values)
    grad_wide = by_heads(cotangent)
    wide_float = jnp.float32
    causal = jnp.tril(jnp.ones((length, length), jnp.float32))
    scores = jnp.einsum("blhe,bmhe->bhlm", query_wide, key_wide, preferred_element_type=wide_float)
    scores = (scores * causal).astype(jnp.bfloat16)
    grad_scores = jnp.einsum(
        "blhf,bmhf->bhlm", grad_wide, value_wide, preferred_element_type=wide_float
    )
    grad_scores = (grad_scores * causal).astype(jnp.bfloat16)
    own_memory = jnp.einsum(
        "blhe,blhf->bhef", key_wide, value_wide, preferred_element_type=wide_float
    )
    own_adjoint = jnp.einsum(
        "blhe,blhf->bhef", query_wide, grad_wide, preferred_element_type=wide_float
    )
    zeroes = jnp.zeros_like(own_memory)
    before = entering(own_memory, "ctx", add_states, zeroes, False)
    later_adjoint = entering(own_adjoint, "ctx", add_states, zeroes, True)
    query_float = query_wide.astype(jnp.float32)
    key_float = key_wide.astype(jnp.float32)
    value_float = value_wide.astype(jnp.float32)
    grad_float = grad_wide.astype(jnp.float32)
    output = jnp.einsum("bhlm,bmhf->blhf", scores, value_wide, preferred_element_type=wide_float)
    output = output + jnp.einsum("blhe,bhef->blhf", query_float, before, precision=exact_mode)
    query_grad = jnp.einsum(
        "bhlm,bmhe->blhe", grad_scores, key_wide, preferred_element_type=wide_float
    )
    query_grad = query_grad + jnp.einsum(
        "blhf,bhef->blhe", grad_float, before, precision=exact_mode
    )
    key_grad = jnp.einsum(
        "bhlm,blhe->bmhe", grad_scores, query_wide, preferred_element_type=wide_float
    )
    key_grad = key_grad + jnp.einsum(
        "bmhf,bhef->bmhe", value_float, later_adjoint, precision=exact_mode
    )
    value_grad = jnp.einsum("bhlm,blhf->bmhf", scores, grad_wide, preferred_element_type=wide_float)
    value_grad = value_grad + jnp.einsum(
        "bmhe,bhef->bmhf", key_float, later_adjoint, precision=exact_mode
    )
    shape_out = (batches, length, head_total)
    attended = (factor * output.reshape(shape_out)).astype(jnp.bfloat16)
    masked_grad = (factor * query_grad.reshape(shape_out) * q_spikes.astype(jnp.float32)).astype(
        jnp.bfloat16
    )
    masked_rows = masked_grad.reshape(batches * length, head_total)
    contract = (((1,), (1,)), ((), ()))
    token_grad = lax.dot_general(
        masked_rows,
        lax.all_gather(q_weight, ("ctx", "dp"), axis=0, tiled=True),
        contract,
        preferred_element_type=jnp.float32,
    )
    grad_tokens = token_grad.reshape(batches, length, model_width).astype(jnp.bfloat16)
    grad_keys = (factor * key_grad.reshape(shape_out) * k_spikes.astype(jnp.float32)).astype(
        jnp.bfloat16
    )
    grad_values = (factor * value_grad.reshape(shape_out)).astype(jnp.bfloat16)
    return (attended, grad_tokens, grad_keys, grad_values)


def solution(mesh):
    in_specs = (
        P("dp", "ctx", None),
        P("dp", "ctx", None),
        P("dp", "ctx", None),
        P(("ctx", "dp"), None),
        P("dp", "ctx", None),
        P("dp", "ctx", None),
        P("dp", "ctx", None),
    )
    out_specs = (
        P("dp", "ctx", None),
        P("dp", "ctx", None),
        P("dp", "ctx", None),
        P("dp", "ctx", None),
    )
    return jax.shard_map(
        per_device, mesh=mesh, in_specs=in_specs, out_specs=out_specs, check_vma=False
    )
```

profile of v0, /device:TPU:1, one launch (start us, length us, event | category | flops | bytes accessed | tf_op | source)
XLA Modules:
  0.0 1037.3 jit_solution(814727491231652069)
XLA Ops:
  8.0 2.7 multiply_bitcast_fusion
  12.3 2.8 copy.38
  20.1 2.6 copy.63
  22.7 204.0 %all-gather.6.cloned.1.call-done = bf16[4096,2048]{1,0:T(8,128)(2,1)} async-done(((bf16[32,2048]{1,0:T(8,128)(2,1)}), bf16[4096,2048]{1,0:T(8,128)(2,1)}) %all-gather.6.cloned.1.call-update) | async-done | bytes 16777232 | tf_op jit(solution)/shard_map/all_gather | solution.py:38
  226.6 12.7 %fusion.5 = bf16[1,384,2048]{2,1,0:T(8,128)(2,1)} fusion(s32[1,384,2048]{2,1,0:T(8,128)} %param.15, bf16[4096,2048]{1,0:T(8,128)(2,1)} %all-gather.6.cloned.1.call-done, bf16[1,384,4096]{2,1,0:T(8,128)(2,1)S(1)} %copy-done), kind=kOutput, calls=%fused_computation.13 | convolution fusion | flops 6444810240 | bytes 24641536 | tf_op jit(solution)/shard_map/dot_general | solution.py:36
  241.2 3.4 fusion.28
  244.7 5.7 multiply_convert_fusion
  250.4 4.2 multiply_convert_fusion.1
  254.6 338.1 %all-gather.8.cloned.1.call-done = f32[512,128,128]{2,1,0:T(8,128)} async-done(((f32[16,128,128]{2,1,0:T(8,128)}), f32[512,128,128]{2,1,0:T(8,128)}) %all-gather.8.cloned.1.call-update) | async-done | bytes 33554448 | tf_op jit(solution)/shard_map/all_gather | solution.py:16
  595.3 4.2 fusion.4
  599.5 2.7 copy.57
  602.2 3.0 fusion.18
  605.2 5.7 add_multiply_fusion.1
  610.9 3.6 copy.61
  614.5 13.4 %fusion = bf16[1,384,4096]{2,1,0:T(8,128)(2,1)} fusion(bf16[4096,2048]{1,0:T(8,128)(2,1)} %all-gather.6.cloned.1.call-done, f32[1,384,2048]{2,1,0:T(8,128)} %copy.61, s32[1,384,2048]{2,1,0:T(8,128)} %param.15), kind=kOutput, calls=%fused_computation.5 | convolution fusion | flops 6446383104 | bytes 26214400 | tf_op jit(solution)/shard_map/dot_general | solution.py:99
  627.9 327.8 %all-gather.10.cloned.1.call-done = f32[512,128,128]{2,1,0:T(8,128)} async-done(((f32[16,128,128]{2,1,0:T(8,128)}), f32[512,128,128]{2,1,0:T(8,128)}) %all-gather.10.cloned.1.call-update) | async-done | bytes 33554448 | tf_op jit(solution)/shard_map/all_gather | solution.py:16
  955.8 47.1 %while.23 = (s32[]{:T(128)}, f32[1,16,128,128]{3,2,1,0:T(8,128)S(1)}, s32[]{:T(128)}, f32[32,1,16,128,128]{4,3,2,1,0:T(8,128)}, s32[]{:T(128)}, /*index=5*/s32[]{:T(128)}, s32[]{:T(128)}, s32[]{:T(128)}) while((s32[]{:T(128)}, f32[1,16,128,128]{3,2,1,0:T(8,128)S(1)}, s32[]{:T(128)}, f32[32,1,16,128,128]{4,3,2,1,0:T(8,128)}, s32[]{:T(128)}, ...), condition=%wide.region_3.4_spmd, body=%wide.region_2.3_spmd.sunk | while | flops 262150 | bytes 3145871 | solution.py:23
  1002.9 3.6 fusion.16
  1006.5 3.7 fusion.12
  1010.2 5.3 add_multiply_fusion
  1015.6 3.8 copy.53
  1019.4 3.9 multiply_convert_fusion.2
  1023.3 4.9 fusion.2
  1028.1 2.6 copy.58
  (70 shorter events, 58.1 us)
Async XLA Ops:
  7.2 219.5 %copy-start = (bf16[1,384,4096]{2,1,0:T(8,128)(2,1)S(1)}, bf16[1,384,4096]{2,1,0:T(8,128)(2,1)}, u32[]{:S(2)}) copy-start(bf16[1,384,4096]{2,1,0:T(8,128)(2,1)} %param.11) | copy-start | bytes 9437188
  7.2 219.5 %all-gather.6.cloned.1.call-start = ((), (), s32[]{:S(2)}) async-start(), calls=%async_computation | async-start | bytes 16908288 | tf_op jit(solution)/shard_map/all_gather | solution.py:38
  7.9 584.8 %all-gather.8.cloned.1.call-start = ((), (), s32[]{:S(2)}) async-start(), calls=%async_computation.1 | async-start | bytes 34603008 | tf_op jit(solution)/shard_map/all_gather | solution.py:16
  15.1 3.1 copy-start.8
  17.0 1.2 copy-start.3
  20.0 935.6 %all-gather.10.cloned.1.call-start = ((), (), s32[]{:S(2)}) async-start(), calls=%async_computation.2 | async-start | bytes 34603008 | tf_op jit(solution)/shard_map/all_gather | solution.py:16
  241.2 3.5 copy-start.4
  244.7 5.8 copy-start.6
  593.0 2.3 copy-start.2
  602.2 3.0 copy-start.9
  1002.9 3.6 copy-start.7
  1015.6 3.8 copy-start.10
  1019.4 3.9 copy-start.5
  1019.4 3.9 copy-start.11
  1023.3 7.5 copy-start.1
Sparse Core Ops, SparseCore 0:
  9.7 216.8 all-gather.5
  228.9 363.7 all-gather.7
  594.3 361.3 all-gather.9
where the time goes:
time: 1040 us
  waiting for transfers between devices  870 us (84%)
  matrix products  73 us (7%)
  other arithmetic  52.8 us (5%)
  local copies, waits for them, and re-layouts  25.8 us (2%)
  between operations  13.9 us (1%)
    all_gather x2, waiting for transfers between devices, entering(): gathered = lax.all_gather(part, axis)  666 us
    all_gather x1, waiting for transfers between devices, per_device(): lax.all_gather(q_weight, ('ctx', 'dp'), axis=0, tiled=True)  204 us
    add x31, other arithmetic, add_states(): return first_part + second_part  46.2 us
  transfers between devices with their start and end apart: 3, of which 3 were waited for; matrix products, arithmetic and copies ran while one was open for 7% of the time, Pallas kernels for 0%

commit v1 on v0

--- a/solution.py
+++ b/solution.py
@@ -7,6 +7,18 @@
 HEADS = 16
 HEAD = 128
 exact_mode = lax.Precision.HIGHEST
+
+
+def packet_serve(t0):
+    return jnp.concatenate(
+        lax.all_to_all(
+            jnp.stack([t0] * lax.axis_size(("ctx", "dp")), 0),
+            ("ctx", "dp"),
+            split_axis=0,
+            concat_axis=0,
+        ),
+        0,
+    )
 
 
 def entering(part, axis, combine, identity, reverse):
@@ -33,11 +45,7 @@
     sequence = length * lax.axis_size("ctx")
     factor = 3.0 / math.sqrt(HEAD * sequence)
     token_rows = tokens.reshape(batches * length, model_width)
-    projected = jnp.dot(
-        token_rows,
-        lax.all_gather(q_weight, ("ctx", "dp"), axis=0, tiled=True),
-        preferred_element_type=jnp.float32,
-    )
+    projected = jnp.dot(token_rows, packet_serve(q_weight), preferred_element_type=jnp.float32)
     queries = (
         projected.reshape(batches, length, head_total) * q_spikes.astype(jnp.float32)
     ).astype(jnp.bfloat16)

time: 1040 us -> 1240 us (1.19)
  waiting for transfers between devices: 870 us -> 1060 us
    all_to_all x0 -> x1, waiting for transfers between devices: none -> 541 us  [packet_serve(): lax.all_to_all(jnp.stack([t0] * lax.axis_size(('ctx', 'dp')), 0), ('ctx',...]
    all_gather x2, waiting for transfers between devices: 666 us -> 352 us  [entering(): gathered = lax.all_gather(part, axis)]
    all_gather x1, waiting for transfers between devices: 204 us -> 164 us  [per_device(): lax.all_gather(q_weight, ('ctx', 'dp'), axis=0, tiled=True)]
  transfers between devices with their start and end apart: 3 -> 4, of which waited for: 3 -> 3; matrix products, arithmetic and copies ran while one was open for 7% -> 6% of each run, Pallas kernels for 0% -> 0%
where the time goes in v1:
time: 1240 us
  waiting for transfers between devices  1060 us (85%)
  matrix products  74.6 us (6%)
  other arithmetic  51.7 us (4%)
  local copies, waits for them, and re-layouts  30 us (2%)
  between operations  13.9 us (1%)
    all_to_all x1, waiting for transfers between devices, packet_serve(): lax.all_to_all(jnp.stack([t0] * lax.axis_size(('ctx', 'dp')), 0), ('ctx',...  541 us
    all_gather x2, waiting for transfers between devices, entering(): gathered = lax.all_gather(part, axis)  352 us
    all_gather x1, waiting for transfers between devices, per_device(): lax.all_gather(q_weight, ('ctx', 'dp'), axis=0, tiled=True)  164 us
    add x31, other arithmetic, add_states(): return first_part + second_part  46.1 us
  transfers between devices with their start and end apart: 4, of which 3 were waited for; matrix products, arithmetic and copies ran while one was open for 6% of the time, Pallas kernels for 0%

profile of v1, /device:TPU:1, one launch (start us, length us, event | category | flops | bytes accessed | tf_op | source)
XLA Modules:
  0.0 1242.5 jit_solution(2014253197680028805)
XLA Ops:
  7.2 3.2 copy.65
  13.7 2.8 copy.38
  16.5 3.7 fusion.25
  21.0 6.1 stack.2
  27.1 12.0 all-to-all-start
  41.7 541.5 %all-to-all-done = bf16[128,32,2048]{2,1,0:T(8,128)(2,1)} async-done(((bf16[128,32,2048]{2,1,0:T(8,128)(2,1)}), bf16[128,32,2048]{2,1,0:T(8,128)(2,1)}, u32[]{:S(2)}, u32[]{:S(2)}) %all-to-all-start) | async-done | bytes 16777248 | tf_op jit(solution)/shard_map/all_to_all | solution.py:14
  583.2 12.7 %fusion.5 = bf16[1,384,2048]{2,1,0:T(8,128)(2,1)} fusion(s32[1,384,2048]{2,1,0:T(8,128)} %param.15, bf16[4096,2048]{1,0:T(8,128)(2,1)} %bitcast.3, bf16[1,384,4096]{2,1,0:T(8,128)(2,1)S(1)} %copy-done), kind=kOutput, calls=%fused_computation.13 | convolution fusion | flops 6444810240 | bytes 24641536 | tf_op jit(solution)/shard_map/dot_general | solution.py:48
  597.8 3.3 fusion.28
  601.2 5.8 multiply_convert_fusion
  607.0 4.2 multiply_convert_fusion.1
  611.5 3.0 fusion.18
  614.5 5.7 add_multiply_fusion.1
  620.3 3.7 copy.61
  625.4 4.0 fusion.4
  631.1 164.1 %all-gather.6.cloned.1.call-done = bf16[4096,2048]{1,0:T(8,128)(2,1)} async-done(((bf16[32,2048]{1,0:T(8,128)(2,1)}), bf16[4096,2048]{1,0:T(8,128)(2,1)}) %all-gather.6.cloned.1.call-update) | async-done | bytes 16777232 | tf_op jit(solution)/shard_map/all_gather | solution.py:109
  795.2 13.2 %fusion = bf16[1,384,4096]{2,1,0:T(8,128)(2,1)} fusion(bf16[4096,2048]{1,0:T(8,128)(2,1)} %all-gather.6.cloned.1.call-done, f32[1,384,2048]{2,1,0:T(8,128)} %copy.61, s32[1,384,2048]{2,1,0:T(8,128)} %param.15), kind=kOutput, calls=%fused_computation.5 | convolution fusion | flops 6446383104 | bytes 26214400 | tf_op jit(solution)/shard_map/dot_general | solution.py:107
  808.4 352.5 %all-gather.10.cloned.1.call-done = f32[512,128,128]{2,1,0:T(8,128)} async-done(((f32[16,128,128]{2,1,0:T(8,128)}), f32[512,128,128]{2,1,0:T(8,128)}) %all-gather.10.cloned.1.call-update) | async-done | bytes 33554448 | tf_op jit(solution)/shard_map/all_gather | solution.py:28
  1161.0 47.2 %while.23 = (s32[]{:T(128)}, f32[1,16,128,128]{3,2,1,0:T(8,128)S(1)}, s32[]{:T(128)}, f32[32,1,16,128,128]{4,3,2,1,0:T(8,128)}, s32[]{:T(128)}, /*index=5*/s32[]{:T(128)}, s32[]{:T(128)}, s32[]{:T(128)}) while((s32[]{:T(128)}, f32[1,16,128,128]{3,2,1,0:T(8,128)S(1)}, s32[]{:T(128)}, f32[32,1,16,128,128]{4,3,2,1,0:T(8,128)}, s32[]{:T(128)}, ...), condition=%wide.region_3.4_spmd, body=%wide.region_2.3_spmd.sunk | while | flops 262150 | bytes 3145863 | solution.py:35
  1208.2 3.6 fusion.16
  1211.8 3.7 fusion.12
  1215.6 5.3 add_multiply_fusion
  1220.9 3.7 copy.53
  1224.7 3.9 multiply_convert_fusion.2
  1228.6 4.9 fusion.2
  (73 shorter events, 60.8 us)
Async XLA Ops:
  7.2 576.0 %copy-start = (bf16[1,384,4096]{2,1,0:T(8,128)(2,1)S(1)}, bf16[1,384,4096]{2,1,0:T(8,128)(2,1)}, u32[]{:S(2)}) copy-start(bf16[1,384,4096]{2,1,0:T(8,128)(2,1)} %param.11) | copy-start | bytes 9437188
  7.2 604.0 %all-gather.8.cloned.1.call-start = ((), (), s32[]{:S(2)}) async-start(), calls=%async_computation.2 | async-start | bytes 34603008 | tf_op jit(solution)/shard_map/all_gather | solution.py:28
  7.2 3.2 copy-start.8
  16.5 4.5 copy-start.11
  20.2 774.9 %all-gather.6.cloned.1.call-start = ((), (), s32[]{:S(2)}) async-start(), calls=%async_computation.1 | async-start | bytes 16908288 | tf_op jit(solution)/shard_map/all_gather | solution.py:109
  27.1 556.1 %all-to-all-start = ((bf16[128,32,2048]{2,1,0:T(8,128)(2,1)}), bf16[128,32,2048]{2,1,0:T(8,128)(2,1)}, u32[]{:S(2)}, u32[]{:S(2)}) async-start(bf16[128,32,2048]{2,1,0:T(8,128)(2,1)} %stack.2), calls=%async_computation | async-start | bytes 33554432 | tf_op jit(solution)/shard_map/all_to_all | solution.py:14
  39.1 1121.8 %all-gather.10.cloned.1.call-start = ((), (), s32[]{:S(2)}) async-start(), calls=%async_computation.3 | async-start | bytes 34603008 | tf_op jit(solution)/shard_map/all_gather | solution.py:28
  597.8 3.4 copy-start.2
  601.2 5.8 copy-start.5
  611.5 3.0 copy-start.7
  623.9 1.4 copy-start.3
  1208.2 3.6 copy-start.6
  1220.9 3.7 copy-start.9
  1224.7 3.9 copy-start.4
  1224.7 3.9 copy-start.10
  1228.6 7.5 copy-start.1
Sparse Core Ops, SparseCore 0:
  20.3 555.5 all-gather.7
  577.6 217.4 all-gather.5
  797.4 363.4 all-gather.9
